TPU v7x, 32 devices: a whole 2x2x4 slice. The times are simulated.
32 devices in a mesh: mem: 2 (over x), col: 16 (over z, y, core).
Axes of the slice: x: 2, y: 2, z: 4, core: 2. Of those that a mesh axis runs over, the one named last changes fastest.
Arguments:
- perturbations: bfloat16 [2, 16, 384, 768], P('mem', None, 'col'), may hold values from -6 to 6
- gradient: float32 [16, 384, 768], P(None, 'col'), may hold values from -6 to 6
- member_weights: float32 [2], P('mem'), may hold values from 0.5 to 2
- scale_weights: float32 [3], replicated, may hold values from 0.2 to 2
- lon_filter: bfloat16 [3, 768, 768], P(None, 'mem'), may hold values from -1 to 1.5
- lat_filter: bfloat16 [3, 384, 384], P(None, 'col'), may hold values from -1 to 1.5
Outputs:
- increment: float32 [16, 384, 768], P('mem', 'col')
All inputs are finite; a program needn't handle non-finite values.
Results may differ from a plain program's by a relative error of at most 0.01.
Values may be sent and summed in bfloat16 or wider, within the bound.
A program may use at most 64 MiB of HBM per device.

v0:
```python
import jax
import jax.numpy as jnp
from jax import lax
from jax.sharding import PartitionSpec as P


def on_device(perturbations, gradient, member_weights, scale_weights, lon_filter, lat_filter):
    member = perturbations[0].astype(jnp.float32)
    schur = (member * gradient).astype(jnp.bfloat16)
    levels = lax.all_to_all(schur, "col", split_axis=0, concat_axis=1, tiled=True)
    along = jnp.einsum(
        "laj,sij->lsai",
        levels,
        lax.all_gather(lon_filter, "mem", axis=1, tiled=True),
        preferred_element_type=jnp.float32,
    ).astype(jnp.bfloat16)
    across = jnp.einsum(
        "sab,lsbi->lsai",
        lax.all_gather(lat_filter, "col", axis=1, tiled=True),
        along,
        preferred_element_type=jnp.float32,
    )
    filtered = jnp.einsum("s,lsai->lai", scale_weights, across).astype(jnp.bfloat16)
    back = lax.all_to_all(filtered, "col", split_axis=1, concat_axis=0, tiled=True)
    terms = member_weights[0] * member * back.astype(jnp.float32)
    return lax.psum_scatter(terms, "mem", scatter_dimension=0, tiled=True)


def solution(mesh):
    placed = (
        P("mem", None, "col", None),
        P(None, "col", None),
        P("mem"),
        P(),
        P(None, "mem", None),
        P(None, "col", None),
    )
    return jax.shard_map(
        on_device, mesh=mesh, in_specs=placed, out_specs=P("mem", "col", None), check_vma=False
    )
```

profile of v0, /device:TPU:0, one launch (start us, length us, event | category | flops | bytes accessed | tf_op | source)
XLA Modules:
  0.0 129.6 jit_solution(12170853550535788724)
XLA Ops:
  6.5 0.0 copy-start
  6.5 0.0 copy-start.1
  6.5 0.0 copy-start.2
  6.5 0.0 all-gather.2.cloned.1.call-start
  6.5 0.7 all-gather.2.cloned.1.call-update
  7.3 0.4 copy-done.1
  7.6 0.4 copy-done.2
  8.0 0.0 copy-start.3
  8.0 0.9 fusion.5
  8.9 7.4 %all-to-all-start = ((bf16[16,24,768]{2,1,0:T(8,128)(2,1)}), bf16[16,24,768]{2,1,0:T(8,128)(2,1)S(1)}, u32[]{:S(2)}, u32[]{:S(2)}) async-start(bf16[16,24,768]{2,1,0:T(8,128)(2,1)} %fusion.5), calls=%async_computation | async-start | bytes 1179648 | tf_op jit(solution)/shard_map/all_to_all | solution.py:10
  16.4 0.0 copy-done.3
  16.4 29.1 %all_gather.7 = bf16[3,384,384]{2,1,0:T(8,128)(2,1)S(1)} all-gather(bf16[3,24,384]{2,1,0:T(8,128)(2,1)S(1)} %copy-done.3), channel_id=1, replica_groups=mesh['mem'=2,'col'=16] {'col'}, dimensions={1}, use_global_device_ids=true | all-gather | bytes 940032 | tf_op jit(solution)/shard_map/all_gather | solution.py:19
  45.5 0.0 all-to-all-done
  45.5 15.5 %all-gather.2.cloned.1.call-done = bf16[3,768,768]{2,1,0:T(8,128)(2,1)} async-done(((bf16[3,384,768]{2,1,0:T(8,128)(2,1)}), bf16[3,768,768]{2,1,0:T(8,128)(2,1)}) %all-gather.2.cloned.1.call-update) | async-done | bytes 3538960 | tf_op jit(solution)/shard_map/all_gather | solution.py:14
  61.0 5.9 %convolution_bitcast_fusion = bf16[3,384,768]{1,2,0:T(8,128)(2,1)} fusion(bf16[3,384,384]{2,1,0:T(8,128)(2,1)S(1)} %all_gather.7, bf16[384,768,1]{1,0,2:T(8,128)(2,1)S(1)} %bitcast.56, bf16[3,768,768]{2,1,0:T(8,128)(2,1)} %all-gather.2.cloned.1.call-done), kind=kOutput, calls=%fused_computation | convolution fusion | flops 2039316480 | bytes 6782976 | tf_op jit(solution)/shard_map/sab,lsbi->lsai/dot_general | solution.py:17
  66.9 4.0 %copy.12 = bf16[3,384,768]{2,0,1:T(4,128)(2,1)S(1)} copy(bf16[3,384,768]{1,2,0:T(8,128)(2,1)} %convolution_bitcast_fusion) | data formatting | bytes 3538944 | tf_op jit(solution)/shard_map/reshape.6
  70.9 0.0 copy-done
  70.9 1.4 %fusion.10 = bf16[1,384,768]{2,0,1:T(2,128)(2,1)S(1)} fusion(bf16[3,384,768]{2,0,1:T(4,128)(2,1)S(1)} %copy.12, f32[3]{0:T(128)S(1)} %copy-done), kind=kOutput, calls=%fused_computation.13 | convolution fusion | flops 1769472 | bytes 2359308 | tf_op jit(solution)/shard_map/s,lsai->lai/dot_general | solution.py:23
  72.2 0.1 copy.19
  72.3 0.9 copy.20
  73.2 0.5 broadcast
  73.8 4.4 %reduce = bf16[384,768]{1,0:T(8,128)(2,1)S(1)} reduce(bf16[384,1,768]{2,1,0:T(2,128)(2,1)S(1)} %bitcast.54, bf16[]{:T(256)} %broadcast), dimensions={1}, to_apply=%bitcast.51.reduce_sub_computation | reduce | bytes 1179650
  78.1 1.0 reshape.33
  79.1 5.6 %all-to-all-start.1 = ((bf16[16,2,9216]{2,1,0:T(2,128)(2,1)}), bf16[16,2,9216]{2,1,0:T(2,128)(2,1)S(1)}, u32[]{:S(2)}, u32[]{:S(2)}) async-start(bf16[16,2,9216]{2,1,0:T(2,128)(2,1)} %reshape.33), calls=%async_computation.1 | async-start | bytes 1179648 | tf_op jit(solution)/shard_map/all_to_all | solution.py:24
  84.7 0.0 reduce-scatter.2.cloned.1.call-start
  85.4 14.7 %all-to-all-done.1 = bf16[16,2,9216]{2,1,0:T(2,128)(2,1)S(1)} async-done(((bf16[16,2,9216]{2,1,0:T(2,128)(2,1)}), bf16[16,2,9216]{2,1,0:T(2,128)(2,1)S(1)}, u32[]{:S(2)}, u32[]{:S(2)}) %all-to-all-start.1) | async-done | bytes 589856 | tf_op jit(solution)/shard_map/all_to_all | solution.py:24
  100.1 0.5 reshape.34
  100.6 0.1 copy.14
  100.7 1.2 fusion.4
  101.8 0.0 reduce-scatter.2.cloned.1.call-update
  101.9 20.9 %reduce-scatter.2.cloned.1.call-done = f32[8,24,768]{2,1,0:T(8,128)} async-done(((f32[16,24,768]{2,1,0:T(8,128)}), f32[8,24,768]{2,1,0:T(8,128)}) %reduce-scatter.2.cloned.1.call-update) | async-done | bytes 589840 | tf_op jit(solution)/shard_map/reduce_scatter | solution.py:26
Async XLA Ops:
  6.5 64.3 %copy-start = (f32[3]{0:T(128)S(1)}, f32[3]{0:T(128)}, u32[]{:S(2)}) copy-start(f32[3]{0:T(128)} %param.9) | copy-start | bytes 40
  6.5 1.1 copy-start.1
  6.5 1.5 %copy-start.2 = (f32[16,24,768]{2,1,0:T(8,128)S(1)}, f32[16,24,768]{2,1,0:T(8,128)}, u32[]{:S(2)}) copy-start(f32[16,24,768]{2,1,0:T(8,128)} %param.7) | copy-start | bytes 3538948
  6.5 54.4 %all-gather.2.cloned.1.call-start = ((), (), s32[]{:S(2)}) async-start(), calls=%async_computation.3 | async-start | bytes 5308416 | tf_op jit(solution)/shard_map/all_gather | solution.py:14
  8.0 8.4 %copy-start.3 = (bf16[3,24,384]{2,1,0:T(8,128)(2,1)S(1)}, bf16[3,24,384]{2,1,0:T(8,128)(2,1)}, u32[]{:S(2)}) copy-start(bf16[3,24,384]{2,1,0:T(8,128)(2,1)} %param.11) | copy-start | bytes 165892
  8.9 36.5 %all-to-all-start = ((bf16[16,24,768]{2,1,0:T(8,128)(2,1)}), bf16[16,24,768]{2,1,0:T(8,128)(2,1)S(1)}, u32[]{:S(2)}, u32[]{:S(2)}) async-start(bf16[16,24,768]{2,1,0:T(8,128)(2,1)} %fusion.5), calls=%async_computation | async-start | bytes 1179648 | tf_op jit(solution)/shard_map/all_to_all | solution.py:10
  79.1 21.0 %all-to-all-start.1 = ((bf16[16,2,9216]{2,1,0:T(2,128)(2,1)}), bf16[16,2,9216]{2,1,0:T(2,128)(2,1)S(1)}, u32[]{:S(2)}, u32[]{:S(2)}) async-start(bf16[16,2,9216]{2,1,0:T(2,128)(2,1)} %reshape.33), calls=%async_computation.1 | async-start | bytes 1179648 | tf_op jit(solution)/shard_map/all_to_all | solution.py:24
  84.7 38.0 %reduce-scatter.2.cloned.1.call-start = ((), (), s32[]{:S(2)}) async-start(), calls=%async_computation.4 | async-start | bytes 1769472 | tf_op jit(solution)/shard_map/reduce_scatter | solution.py:26
Sparse Core Ops, SparseCore 0:
  8.9 52.0 all-gather.1
  102.0 20.7 reduce-scatter.1
where the time goes:
time: 130 us
  waiting for transfers between devices  51.8 us (40%)
  blocking collectives  29.1 us (22%)
  between operations  14.1 us (11%)
  starting transfers between devices  13.1 us (10%)
  local copies, waits for them, and re-layouts  7.76 us (6%)
  matrix products  7.27 us (6%)
  other arithmetic  6.47 us (5%)
    all_gather x1, blocking collectives, on_device(): lax.all_gather(lat_filter, 'col', axis=1, tiled=True)  29.1 us
    reduce_scatter x1, waiting for transfers between devices, on_device(): return lax.psum_scatter(terms, 'mem', scatter_dimension=0, tiled=True)  20.9 us
    all_gather x1, waiting for transfers between devices, on_device(): lax.all_gather(lon_filter, 'mem', axis=1, tiled=True)  15.5 us
    all_to_all x1, waiting for transfers between devices, on_device(): lax.all_to_all(filtered, 'col', split_axis=1, concat_axis=0, tiled=True)  14.7 us
    all_to_all x1, starting transfers between devices, on_device(): lax.all_to_all(schur, 'col', split_axis=0, concat_axis=1, tiled=True)  7.41 us
    dot_general x1, matrix products, on_device(): jnp.einsum('sab,lsbi->lsai', lax.all_gather(lat_filter, 'col', axis=1, ti...  5.91 us
    all_to_all x1, starting transfers between devices, on_device(): lax.all_to_all(filtered, 'col', split_axis=1, concat_axis=0, tiled=True)  5.62 us
    unnamed x1, other arithmetic  4.37 us
  transfers between devices with their start and end apart: 4, of which 3 were waited for; matrix products, arithmetic and copies ran while one was open for 1% of the time, Pallas kernels for 0%

commit v1 on v0

--- a/solution.py
+++ b/solution.py
@@ -21,7 +21,10 @@
         preferred_element_type=jnp.float32,
     )
     filtered = jnp.einsum("s,lsai->lai", scale_weights, across).astype(jnp.bfloat16)
-    back = lax.all_to_all(filtered, "col", split_axis=1, concat_axis=0, tiled=True)
+    size = lax.axis_size("col")
+    blocks = jnp.stack(jnp.split(filtered, size, axis=1), axis=0)
+    blocks = lax.all_to_all(blocks, "col", split_axis=0, concat_axis=0)
+    back = jnp.concatenate(blocks, axis=0)
     terms = member_weights[0] * member * back.astype(jnp.float32)
     return lax.psum_scatter(terms, "mem", scatter_dimension=0, tiled=True)
 

time: 130 us -> 133 us (1.023)
  local copies, waits for them, and re-layouts: 7.76 us -> 14.7 us
  other arithmetic: 6.47 us -> 2.11 us
    unnamed x12 -> x23, local copies, waits for them, and re-layouts: 2.8 us -> 10 us
    unnamed x1 -> x0, other arithmetic: 4.37 us -> none
    another operation x1 -> x2, local copies, waits for them, and re-layouts: 3.98 us -> 4.6 us
where the time goes in v1:
time: 133 us; the launch traced here: 132 us
  waiting for transfers between devices  51.8 us (39%)
  blocking collectives  29.1 us (22%)
  local copies, waits for them, and re-layouts  14.7 us (11%)
  between operations  14.1 us (11%)
  starting transfers between devices  13.1 us (10%)
  matrix products  7.27 us (5%)
  other arithmetic  2.11 us (2%)
    all_gather x1, blocking collectives, on_device(): lax.all_gather(lat_filter, 'col', axis=1, tiled=True)  29.1 us
    reduce_scatter x1, waiting for transfers between devices, on_device(): return lax.psum_scatter(terms, 'mem', scatter_dimension=0, tiled=True)  20.9 us
    all_gather x1, waiting for transfers between devices, on_device(): lax.all_gather(lon_filter, 'mem', axis=1, tiled=True)  15.5 us
    all_to_all x1, waiting for transfers between devices, on_device(): blocks = lax.all_to_all(blocks, 'col', split_axis=0, concat_axis=0)  14.7 us
    unnamed x23, local copies, waits for them, and re-layouts  10 us
    all_to_all x1, starting transfers between devices, on_device(): lax.all_to_all(schur, 'col', split_axis=0, concat_axis=1, tiled=True)  7.41 us
    dot_general x1, matrix products, on_device(): jnp.einsum('sab,lsbi->lsai', lax.all_gather(lat_filter, 'col', axis=1, ti...  5.91 us
    all_to_all x1, starting transfers between devices, on_device(): blocks = lax.all_to_all(blocks, 'col', split_axis=0, concat_axis=0)  5.62 us
  transfers between devices with their start and end apart: 4, of which 3 were waited for; matrix products, arithmetic and copies ran while one was open for 1% of the time, Pallas kernels for 0%

profile of v1, /device:TPU:0, one launch (start us, length us, event | category | flops | bytes accessed | tf_op | source)
XLA Modules:
  0.0 132.2 jit_solution(2582915562427774391)
XLA Ops:
  6.5 0.7 all-gather.2.cloned.1.call-update
  7.3 0.4 copy-done.1
  7.6 0.4 copy-done.2
  8.0 0.9 fusion.5
  8.9 7.4 %all-to-all-start = ((bf16[16,24,768]{2,1,0:T(8,128)(2,1)}), bf16[16,24,768]{2,1,0:T(8,128)(2,1)S(1)}, u32[]{:S(2)}, u32[]{:S(2)}) async-start(bf16[16,24,768]{2,1,0:T(8,128)(2,1)} %fusion.5), calls=%async_computation | async-start | bytes 1179648 | tf_op jit(solution)/shard_map/all_to_all | solution.py:10
  16.4 29.1 %all_gather.7 = bf16[3,384,384]{2,1,0:T(8,128)(2,1)S(1)} all-gather(bf16[3,24,384]{2,1,0:T(8,128)(2,1)S(1)} %copy-done.3), channel_id=1, replica_groups=mesh['mem'=2,'col'=16] {'col'}, dimensions={1}, use_global_device_ids=true | all-gather | bytes 940032 | tf_op jit(solution)/shard_map/all_gather | solution.py:19
  45.5 15.5 %all-gather.2.cloned.1.call-done = bf16[3,768,768]{2,1,0:T(8,128)(2,1)} async-done(((bf16[3,384,768]{2,1,0:T(8,128)(2,1)}), bf16[3,768,768]{2,1,0:T(8,128)(2,1)}) %all-gather.2.cloned.1.call-update) | async-done | bytes 3538960 | tf_op jit(solution)/shard_map/all_gather | solution.py:14
  61.0 5.9 %convolution_bitcast_fusion = bf16[3,384,768]{1,2,0:T(8,128)(2,1)} fusion(bf16[3,384,384]{2,1,0:T(8,128)(2,1)S(1)} %all_gather.7, bf16[384,768,1]{1,0,2:T(8,128)(2,1)S(1)} %bitcast.115, bf16[3,768,768]{2,1,0:T(8,128)(2,1)} %all-gather.2.cloned.1.call-done), kind=kOutput, calls=%fused_computation | convolution fusion | flops 2039316480 | bytes 6782976 | tf_op jit(solution)/shard_map/sab,lsbi->lsai/dot_general | solution.py:17
  66.9 4.0 %copy.25 = bf16[3,384,768]{2,0,1:T(4,128)(2,1)S(1)} copy(bf16[3,384,768]{1,2,0:T(8,128)(2,1)} %convolution_bitcast_fusion) | data formatting | bytes 3538944 | tf_op jit(solution)/shard_map/reshape.7
  70.9 1.4 %fusion.26 = bf16[1,384,768]{2,0,1:T(2,128)(2,1)S(1)} fusion(bf16[3,384,768]{2,0,1:T(4,128)(2,1)S(1)} %copy.25, f32[3]{0:T(128)S(1)} %copy-done), kind=kOutput, calls=%fused_computation.44 | convolution fusion | flops 1769472 | bytes 2359308 | tf_op jit(solution)/shard_map/s,lsai->lai/dot_general | solution.py:23
  72.3 0.1 copy.30
  72.3 0.6 fusion.22
  73.0 0.6 fusion.21
  73.6 0.6 fusion.20
  74.2 0.6 fusion.19
  74.8 0.6 fusion.18
  75.4 0.6 fusion.17
  76.0 0.6 fusion.16
  76.7 0.6 fusion.15
  77.3 0.6 fusion.14
  77.9 0.6 fusion.13
  78.5 0.6 fusion.12
  79.1 0.6 fusion.11
  79.8 0.6 fusion.10
  80.4 0.6 fusion.9
  81.0 0.6 fusion.8
  81.6 0.6 fusion.7
  82.2 5.6 %all-to-all-start.1 = ((bf16[16,1,24,768]{3,2,1,0:T(8,128)(2,1)}), bf16[16,1,24,768]{3,2,1,0:T(8,128)(2,1)S(1)}, u32[]{:S(2)}, u32[]{:S(2)}) async-start(bf16[16,1,24,768]{3,2,1,0:T(8,128)(2,1)} %fusion.7), calls=%async_computation.1 | async-start | bytes 1179648 | tf_op jit(solution)/shard_map/all_to_all | solution.py:26
  87.9 0.0 reduce-scatter.2.cloned.1.call-start
  88.6 14.7 %all-to-all-done.1 = bf16[16,1,24,768]{3,2,1,0:T(8,128)(2,1)S(1)} async-done(((bf16[16,1,24,768]{3,2,1,0:T(8,128)(2,1)}), bf16[16,1,24,768]{3,2,1,0:T(8,128)(2,1)S(1)}, u32[]{:S(2)}, u32[]{:S(2)}) %all-to-all-start.1) | async-done | bytes 589856 | tf_op jit(solution)/shard_map/all_to_all | solution.py:26
  103.2 1.2 fusion.4
  104.4 20.9 %reduce-scatter.2.cloned.1.call-done = f32[8,24,768]{2,1,0:T(8,128)} async-done(((f32[16,24,768]{2,1,0:T(8,128)}), f32[8,24,768]{2,1,0:T(8,128)}) %reduce-scatter.2.cloned.1.call-update) | async-done | bytes 589840 | tf_op jit(solution)/shard_map/reduce_scatter | solution.py:29
  (9 shorter events, 0.0 us)
Async XLA Ops:
  6.5 64.3 %copy-start = (f32[3]{0:T(128)S(1)}, f32[3]{0:T(128)}, u32[]{:S(2)}) copy-start(f32[3]{0:T(128)} %param.9) | copy-start | bytes 40
  6.5 1.1 copy-start.1
  6.5 1.5 %copy-start.2 = (f32[16,24,768]{2,1,0:T(8,128)S(1)}, f32[16,24,768]{2,1,0:T(8,128)}, u32[]{:S(2)}) copy-start(f32[16,24,768]{2,1,0:T(8,128)} %param.7) | copy-start | bytes 3538948
  6.5 54.4 %all-gather.2.cloned.1.call-start = ((), (), s32[]{:S(2)}) async-start(), calls=%async_computation.3 | async-start | bytes 5308416 | tf_op jit(solution)/shard_map/all_gather | solution.py:14
  8.0 8.4 %copy-start.3 = (bf16[3,24,384]{2,1,0:T(8,128)(2,1)S(1)}, bf16[3,24,384]{2,1,0:T(8,128)(2,1)}, u32[]{:S(2)}) copy-start(bf16[3,24,384]{2,1,0:T(8,128)(2,1)} %param.11) | copy-start | bytes 165892
  8.9 36.5 %all-to-all-start = ((bf16[16,24,768]{2,1,0:T(8,128)(2,1)}), bf16[16,24,768]{2,1,0:T(8,128)(2,1)S(1)}, u32[]{:S(2)}, u32[]{:S(2)}) async-start(bf16[16,24,768]{2,1,0:T(8,128)(2,1)} %fusion.5), calls=%async_computation | async-start | bytes 1179648 | tf_op jit(solution)/shard_map/all_to_all | solution.py:10
  82.2 21.0 %all-to-all-start.1 = ((bf16[16,1,24,768]{3,2,1,0:T(8,128)(2,1)}), bf16[16,1,24,768]{3,2,1,0:T(8,128)(2,1)S(1)}, u32[]{:S(2)}, u32[]{:S(2)}) async-start(bf16[16,1,24,768]{3,2,1,0:T(8,128)(2,1)} %fusion.7), calls=%async_computation.1 | async-start | bytes 1179648 | tf_op jit(solution)/shard_map/all_to_all | solution.py:26
  87.9 37.4 %reduce-scatter.2.cloned.1.call-start = ((), (), s32[]{:S(2)}) async-start(), calls=%async_computation.4 | async-start | bytes 1769472 | tf_op jit(solution)/shard_map/reduce_scatter | solution.py:29
Sparse Core Ops, SparseCore 0:
  8.9 52.0 all-gather.1
  104.6 20.7 reduce-scatter.1
